TPU v7x, 32 devices: a whole 2x2x4 slice. The times are simulated.
32 devices in a mesh: pts: 16 (over z, x, core), modes: 2 (over y).
Axes of the slice: x: 2, y: 2, z: 4, core: 2. Of those that a mesh axis runs over, the one named last changes fastest.
Arguments:
- features: bfloat16 [65536, 128], P('pts'), may hold values from -6 to 6
- coords: float32 [3, 65536], P(None, 'pts'), may hold values from 0 to 1
- quad_weight: float32 [65536], P('pts'), may hold values from 0.5 to 6, as said below
- mode_table: int32 [3, 8192], replicated, may hold values from -8 to 31, as said below
- mode_weight: bfloat16 [8192, 2, 128, 128], P(('pts', 'modes')), may hold values from -4 to 4
- lin_weight: bfloat16 [128, 128], replicated, may hold values from -0.5 to 0.5
- bias: float32 [128], replicated, may hold values from -3 to 3
Outputs:
- output: bfloat16 [65536, 128], P(('pts', 'modes'))
Inputs may be any that keep to these rules, and one draw needn't show every extreme that they name: `mode_table`: each column is a distinct triple (kx, ky, kz) with -8 <= kx < 8, -8 <= ky < 8, 0 <= kz < 32; every such triple appears exactly once, in an order drawn from the seed. `quad_weight`: Positive.
All inputs are finite; a program needn't handle non-finite values.
Results may differ from a plain program's by a relative error of at most 0.018.
Values may be sent and summed in bfloat16 or wider, within the bound.
A program may use at most 128 MiB of HBM per device.

v0:
```python
import math
import jax
import jax.numpy as jnp
from jax import lax
from jax.sharding import PartitionSpec as P


def phase_basis(coords, wave):
    turns = coords[0][:, None] * wave[0][None, :] + coords[1][:, None] * wave[1][None, :]
    turns = turns + coords[2][:, None] * wave[2][None, :]
    angle = 2.0 * math.pi * turns
    return jnp.concatenate([jnp.cos(angle), -jnp.sin(angle)], axis=1).astype(jnp.bfloat16)


def on_device(features, coords, quad_weight, mode_table, mode_weight, lin_weight, bias):
    width = features.shape[1]
    local_pts = features.shape[0]
    own_modes = mode_weight.shape[0]
    n_pts = lax.axis_size("pts")
    n_groups = lax.axis_size("modes")
    group = lax.axis_index("modes")
    group_modes = n_pts * own_modes
    weighted = (quad_weight[:, None] * features.astype(jnp.float32)).astype(jnp.bfloat16)
    total = lax.psum(jnp.sum(quad_weight), "pts")
    wave_all = mode_table.astype(jnp.float32)
    grouped = wave_all.reshape(3, n_pts, n_groups, own_modes)
    wave_group = lax.dynamic_slice_in_dim(grouped, group, 1, 2).reshape(3, group_modes)
    basis_all = phase_basis(coords, wave_group)

    def pick_columns(rows):
        cosine = lax.slice_in_dim(basis_all, 0, rows, axis=1)
        sine = lax.dynamic_slice_in_dim(basis_all, group_modes, rows, 1)
        return jnp.concatenate([cosine, sine], axis=1)

    basis = pick_columns(lax.axis_size("pts") * own_modes)
    term = lax.dot_general(
        basis, weighted, (((0,), (0,)), ((), ())), preferred_element_type=jnp.float32
    )
    coef = lax.psum_scatter(
        term.reshape(2, lax.axis_size("pts") * own_modes, width)
        .transpose(1, 0, 2)
        .reshape(lax.axis_size("pts") * own_modes, 2 * width)
        .astype(jnp.bfloat16),
        "pts",
        scatter_dimension=0,
        tiled=True,
    )
    real_in = coef[:, :width]
    imag_in = coef[:, width:]
    w_real = mode_weight[:, 0]
    w_imag = mode_weight[:, 1]
    real_out = jnp.einsum(
        "mc,mcd->md", real_in, w_real, preferred_element_type=jnp.float32
    ) - jnp.einsum("mc,mcd->md", imag_in, w_imag, preferred_element_type=jnp.float32)
    imag_out = jnp.einsum(
        "mc,mcd->md", real_in, w_imag, preferred_element_type=jnp.float32
    ) + jnp.einsum("mc,mcd->md", imag_in, w_real, preferred_element_type=jnp.float32)
    filtered = jnp.concatenate([real_out, imag_out], axis=1).astype(jnp.bfloat16)
    out_rows = local_pts // n_groups
    my_features = lax.dynamic_slice_in_dim(features, group * out_rows, out_rows, 0)
    piece = lax.all_gather(filtered, "pts", axis=0, tiled=True)
    basis = pick_columns(piece.shape[0])
    rhs = jnp.concatenate([piece[:, :width], piece[:, width:]], axis=0)
    field = jnp.dot(basis, rhs, preferred_element_type=jnp.float32)
    spectral = lax.psum_scatter(
        field.astype(jnp.bfloat16), "modes", scatter_dimension=0, tiled=True
    ).astype(jnp.float32)
    linear = jnp.dot(my_features, lin_weight, preferred_element_type=jnp.float32)
    pre = spectral / total + linear + bias[None, :]
    return jax.nn.gelu(pre, approximate=False).astype(jnp.bfloat16)


def solution(mesh):
    return jax.shard_map(
        on_device,
        mesh=mesh,
        in_specs=(
            P("pts", None),
            P(None, "pts"),
            P("pts"),
            P(),
            P(("pts", "modes"), None, None, None),
            P(),
            P(),
        ),
        out_specs=P(("pts", "modes"), None),
        check_vma=False,
    )
```

profile of v0, /device:TPU:0, one launch (start us, length us, event | category | flops | bytes accessed | tf_op | source)
XLA Modules:
  0.0 505.3 jit_solution(14802626488108388729)
XLA Ops:
  6.5 0.9 convert_element_type.32
  7.5 0.1 reshape.19
  7.6 1.0 fusion.36
  8.6 0.1 constant_dynamic-slice_fusion.1
  8.7 264.3 %cosine_convert_fusion = (bf16[4096,4096]{1,0:T(8,128)(2,1)}, bf16[4096,4096]{1,0:T(8,128)(2,1)}) fusion(f32[4096]{0:T(1024)S(1)} %bitcast.45, f32[4096]{0:T(1024)S(1)} %bitcast.47, f32[4096]{0:T(1024)S(1)} %bitcast.44, f32[4096]{0:T(1024)S(1)} %bitcast.48, f32[4096]{0:T(1024)S(1)} %bitcast.43, f32[4096]{0:T(1024)S(1)} %bitcast.46), kind=kLoop, calls=%fused_computation.2 | loop fusion | flops 150994944 | bytes 67207168 | tf_op jit(solution)/shard_map/convert.2
  273.0 27.4 %fusion.2 = bf16[8192,128]{1,0:T(8,128)(2,1)S(1)} fusion(bf16[4096,4096]{1,0:T(8,128)(2,1)} %get-tuple-element.10, bf16[4096,4096]{1,0:T(8,128)(2,1)} %get-tuple-element.9, bf16[4096,128]{1,0:T(8,128)(2,1)S(1)} %copy-done.2, f32[4096]{0:T(1024)S(1)} %copy-done.1), kind=kOutput, calls=%fused_computation.6 | convolution fusion | flops 8726773760 | bytes 70270976 | tf_op jit(solution)/shard_map/dot_general | solution.py:36
  300.3 2.8 copy.8
  303.2 0.2 all-gather.2.cloned.1.call-start
  303.4 64.5 %reduce-scatter.3.cloned.1.call-done = bf16[256,256]{0,1:T(8,128)(2,1)} async-done(((bf16[4096,256]{0,1:T(8,128)(2,1)}), bf16[256,256]{0,1:T(8,128)(2,1)}) %reduce-scatter.3.cloned.1.call-update) | async-done | bytes 131088 | tf_op jit(solution)/shard_map/reduce_scatter | solution.py:39
  367.9 0.9 slice_bitcast_fusion
  368.8 0.1 copy.9
  368.9 5.7 %fusion.9 = f32[256,1,128]{2,1,0:T(1,128)S(1)} fusion(bf16[256,128,1]{1,2,0:T(2,128)(2,1)S(1)} %copy.9, bf16[256,2,128,128]{3,2,1,0:T(8,128)(2,1)} %param.11), kind=kOutput, calls=%fused_computation.13 | convolution fusion | flops 8388608 | bytes 8585216 | tf_op jit(solution)/shard_map/mc,mcd->md/dot_general | solution.py:52
  374.6 5.7 %fusion.3 = f32[256,1,128]{2,1,0:T(1,128)S(1)} fusion(bf16[256,128,1]{1,2,0:T(2,128)(2,1)S(1)} %copy.9, bf16[256,2,128,128]{3,2,1,0:T(8,128)(2,1)} %param.11), kind=kOutput, calls=%fused_computation.7 | convolution fusion | flops 8388608 | bytes 8585216 | tf_op jit(solution)/shard_map/mc,mcd->md/dot_general | solution.py:55
  380.3 0.1 copy.11
  380.4 5.7 %fusion.5 = f32[256,1,128]{2,1,0:T(1,128)S(1)} fusion(bf16[256,128,1]{1,2,0:T(2,128)(2,1)S(1)} %copy.11, bf16[256,2,128,128]{3,2,1,0:T(8,128)(2,1)} %param.11), kind=kOutput, calls=%fused_computation.9 | convolution fusion | flops 8388608 | bytes 8585216 | tf_op jit(solution)/shard_map/mc,mcd->md/dot_general | solution.py:54
  386.1 5.7 %fusion.7 = f32[256,1,128]{2,1,0:T(1,128)S(1)} fusion(bf16[256,128,1]{1,2,0:T(2,128)(2,1)S(1)} %copy.11, bf16[256,2,128,128]{3,2,1,0:T(8,128)(2,1)} %param.11), kind=kOutput, calls=%fused_computation.11 | convolution fusion | flops 8388608 | bytes 8585216 | tf_op jit(solution)/shard_map/mc,mcd->md/dot_general | solution.py:57
  391.9 0.7 pad_maximum_fusion.7
  392.6 0.0 reduce-scatter.5.cloned.1.call-start
  392.6 40.5 %all-gather.2.cloned.1.call-done = bf16[4096,256]{1,0:T(8,128)(2,1)} async-done(((bf16[256,256]{1,0:T(8,128)(2,1)}), bf16[4096,256]{1,0:T(8,128)(2,1)}) %all-gather.2.cloned.1.call-update) | async-done | bytes 2097168 | tf_op jit(solution)/shard_map/all_gather | solution.py:61
  433.1 1.7 fusion.35
  434.8 26.5 %fusion.15 = bf16[4096,128]{1,0:T(8,128)(2,1)} fusion(bf16[4096,4096]{1,0:T(8,128)(2,1)} %get-tuple-element.10, bf16[4096,4096]{1,0:T(8,128)(2,1)} %get-tuple-element.9, bf16[4096,128]{1,0:T(8,128)(2,1)S(1)} %get-tuple-element.6, bf16[4096,128]{1,0:T(8,128)(2,1)S(1)} %get-tuple-element.5), kind=kOutput, calls=%fused_computation.19 | convolution fusion | flops 8728870912 | bytes 70254592 | tf_op jit(solution)/shard_map/dot_general | solution.py:64
  461.3 0.6 reduce_sum.9
  461.9 32.0 %psum.7 = f32[]{:T(128)} all-reduce(f32[]{:T(128)} %reduce_sum.9), channel_id=1, replica_groups=mesh['pts'=16,'modes'=2] {'pts'}, use_global_device_ids=true, to_apply=%region_3.0 | all-reduce | flops 1 | bytes 8 | tf_op jit(solution)/shard_map/psum | solution.py:24
  493.9 4.9 fusion.22
  (14 shorter events, 0.1 us)
Async XLA Ops:
  6.5 487.3 %copy-start = (bf16[128,128]{1,0:T(8,128)(2,1)S(1)}, bf16[128,128]{1,0:T(8,128)(2,1)}, u32[]{:S(2)}) copy-start(bf16[128,128]{1,0:T(8,128)(2,1)} %param.12) | copy-start | bytes 98308
  6.5 361.4 %reduce-scatter.3.cloned.1.call-start = ((), (), s32[]{:S(2)}) async-start(), calls=%async_computation.2 | async-start | bytes 2228224 | tf_op jit(solution)/shard_map/reduce_scatter | solution.py:39
  8.7 264.3 %copy-start.1 = (f32[4096]{0:T(1024)S(1)}, f32[4096]{0:T(1024)}, u32[]{:S(2)}) copy-start(f32[4096]{0:T(1024)} %param.9) | copy-start | bytes 49156
  8.7 264.3 %copy-start.2 = (bf16[4096,128]{1,0:T(8,128)(2,1)S(1)}, bf16[4096,128]{1,0:T(8,128)(2,1)}, u32[]{:S(2)}) copy-start(bf16[4096,128]{1,0:T(8,128)(2,1)} %param.7) | copy-start | bytes 3145732
  303.2 129.9 %all-gather.2.cloned.1.call-start = ((), (), s32[]{:S(2)}) async-start(), calls=%async_computation.3 | async-start | bytes 2228224 | tf_op jit(solution)/shard_map/all_gather | solution.py:61
  392.6 101.3 %reduce-scatter.5.cloned.1.call-start = ((), (), s32[]{:S(2)}) async-start(), calls=%async_computation.4 | async-start | bytes 1572864 | tf_op jit(solution)/shard_map/reduce_scatter | solution.py:65
  434.8 59.1 %copy-start.3 = (f32[128]{0:T(128)S(1)}, f32[128]{0:T(128)}, u32[]{:S(2)}) copy-start(f32[128]{0:T(128)} %param.13) | copy-start | bytes 1540
Sparse Core Ops, SparseCore 0:
  303.3 64.5 reduce-scatter.2
  392.7 40.3 all-gather.1
  461.4 19.1 reduce-scatter.4
where the time goes:
time: 506 us; the launch traced here: 505 us
  other arithmetic  267 us (53%)
  waiting for transfers between devices  105 us (21%)
  matrix products  81.5 us (16%)
  blocking collectives  32 us (6%)
  between operations  13.2 us (3%)
  local copies, waits for them, and re-layouts  6.8 us (1%)
    another operation x2, other arithmetic  264 us
    reduce_scatter x1, waiting for transfers between devices, on_device(): lax.psum_scatter(term.reshape(2, lax.axis_size('pts') * own_modes, width)...  64.5 us
    all_gather x1, waiting for transfers between devices, on_device(): piece = lax.all_gather(filtered, 'pts', axis=0, tiled=True)  40.5 us
    psum x1, blocking collectives, on_device(): total = lax.psum(jnp.sum(quad_weight), 'pts')  32 us
    dot_general x1, matrix products, on_device(): lax.dot_general(basis, weighted, (((0,), (0,)), ((), ())), preferred_elem...  27.4 us
    dot_general x1, matrix products, on_device(): field = jnp.dot(basis, rhs, preferred_element_type=jnp.float32)  26.5 us
  transfers between devices with their start and end apart: 3, of which 2 were waited for; matrix products, arithmetic and copies ran while one was open for 0% of the time, Pallas kernels for 0%

commit v1 on v0

--- a/solution.py
+++ b/solution.py
@@ -58,7 +58,9 @@
     filtered = jnp.concatenate([real_out, imag_out], axis=1).astype(jnp.bfloat16)
     out_rows = local_pts // n_groups
     my_features = lax.dynamic_slice_in_dim(features, group * out_rows, out_rows, 0)
-    piece = lax.all_gather(filtered, "pts", axis=0, tiled=True)
+    piece = jnp.concatenate(
+        lax.all_to_all(jnp.stack([filtered] * lax.axis_size("pts")), "pts", 0, 0), axis=0
+    )
     basis = pick_columns(piece.shape[0])
     rhs = jnp.concatenate([piece[:, :width], piece[:, width:]], axis=0)
     field = jnp.dot(basis, rhs, preferred_element_type=jnp.float32)

time: 506 us -> 516 us (1.020)
  blocking collectives: 32 us -> 84.5 us
  waiting for transfers between devices: 105 us -> 64.5 us
    all_to_all x0 -> x1, blocking collectives: none -> 50.6 us  [on_device(): lax.all_to_all(jnp.stack([filtered] * lax.axis_size('pts')), 'pts', 0, 0)]
    all_gather x1 -> x0, waiting for transfers between devices: 40.5 us -> none  [on_device(): piece = lax.all_gather(filtered, 'pts', axis=0, tiled=True)]
  transfers between devices with their start and end apart: 3 -> 2, of which waited for: 2 -> 1; matrix products, arithmetic and copies ran while one was open for 0% -> 0% of each run, Pallas kernels for 0% -> 0%
where the time goes in v1:
time: 516 us
  other arithmetic  266 us (52%)
  blocking collectives  84.5 us (16%)
  matrix products  81.6 us (16%)
  waiting for transfers between devices  64.5 us (12%)
  between operations  13.5 us (3%)
  local copies, waits for them, and re-layouts  5.43 us (1%)
    another operation x2, other arithmetic  264 us
    reduce_scatter x1, waiting for transfers between devices, on_device(): lax.psum_scatter(term.reshape(2, lax.axis_size('pts') * own_modes, width)...  64.5 us
    all_to_all x1, blocking collectives, on_device(): lax.all_to_all(jnp.stack([filtered] * lax.axis_size('pts')), 'pts', 0, 0)  50.6 us
    psum x1, blocking collectives, on_device(): total = lax.psum(jnp.sum(quad_weight), 'pts')  33.9 us
    dot_general x1, matrix products, on_device(): lax.dot_general(basis, weighted, (((0,), (0,)), ((), ())), preferred_elem...  27.4 us
    dot_general x1, matrix products, on_device(): field = jnp.dot(basis, rhs, preferred_element_type=jnp.float32)  26.5 us
  transfers between devices with their start and end apart: 2, of which 1 were waited for; matrix products, arithmetic and copies ran while one was open for 0% of the time, Pallas kernels for 0%

profile of v1, /device:TPU:0, one launch (start us, length us, event | category | flops | bytes accessed | tf_op | source)
XLA Modules:
  0.0 515.6 jit_solution(15989069221392253036)
XLA Ops:
  6.5 0.9 convert_element_type.34
  7.5 0.1 reshape.29
  7.6 1.0 fusion.36
  8.6 0.1 constant_dynamic-slice_fusion.1
  8.7 264.2 %cosine_convert_fusion = (bf16[4096,4096]{1,0:T(8,128)(2,1)}, bf16[4096,4096]{1,0:T(8,128)(2,1)}) fusion(f32[4096]{0:T(1024)S(1)} %bitcast.47, f32[4096]{0:T(1024)S(1)} %bitcast.49, f32[4096]{0:T(1024)S(1)} %bitcast.46, f32[4096]{0:T(1024)S(1)} %bitcast.50, f32[4096]{0:T(1024)S(1)} %bitcast.45, f32[4096]{0:T(1024)S(1)} %bitcast.48), kind=kLoop, calls=%fused_computation.2 | loop fusion | flops 150994944 | bytes 67207168 | tf_op jit(solution)/shard_map/convert.2
  272.9 27.4 %fusion.2 = bf16[8192,128]{1,0:T(8,128)(2,1)S(1)} fusion(bf16[4096,4096]{1,0:T(8,128)(2,1)} %get-tuple-element.10, bf16[4096,4096]{1,0:T(8,128)(2,1)} %get-tuple-element.9, bf16[4096,128]{1,0:T(8,128)(2,1)S(1)} %copy-done.2, f32[4096]{0:T(1024)S(1)} %copy-done.1), kind=kOutput, calls=%fused_computation.6 | convolution fusion | flops 8726773760 | bytes 70270976 | tf_op jit(solution)/shard_map/dot_general | solution.py:36
  300.3 2.8 copy.8
  303.1 0.0 reduce-scatter.3.cloned.1.call-update
  303.1 0.2 reduce-scatter.5.cloned.1.call-start
  303.3 64.5 %reduce-scatter.3.cloned.1.call-done = bf16[256,256]{0,1:T(8,128)(2,1)} async-done(((bf16[4096,256]{0,1:T(8,128)(2,1)}), bf16[256,256]{0,1:T(8,128)(2,1)}) %reduce-scatter.3.cloned.1.call-update) | async-done | bytes 131088 | tf_op jit(solution)/shard_map/reduce_scatter | solution.py:39
  367.8 0.9 slice_bitcast_fusion
  368.7 0.1 copy.9
  368.8 5.7 %fusion.9 = f32[256,1,128]{2,1,0:T(1,128)S(1)} fusion(bf16[256,128,1]{1,2,0:T(2,128)(2,1)S(1)} %copy.9, bf16[256,2,128,128]{3,2,1,0:T(8,128)(2,1)} %param.11), kind=kOutput, calls=%fused_computation.13 | convolution fusion | flops 8388608 | bytes 8585216 | tf_op jit(solution)/shard_map/mc,mcd->md/dot_general | solution.py:52
  374.5 5.7 %fusion.3 = f32[256,1,128]{2,1,0:T(1,128)S(1)} fusion(bf16[256,128,1]{1,2,0:T(2,128)(2,1)S(1)} %copy.9, bf16[256,2,128,128]{3,2,1,0:T(8,128)(2,1)} %param.11), kind=kOutput, calls=%fused_computation.7 | convolution fusion | flops 8388608 | bytes 8585216 | tf_op jit(solution)/shard_map/mc,mcd->md/dot_general | solution.py:55
  380.2 0.1 copy.11
  380.3 5.7 %fusion.5 = f32[256,1,128]{2,1,0:T(1,128)S(1)} fusion(bf16[256,128,1]{1,2,0:T(2,128)(2,1)S(1)} %copy.11, bf16[256,2,128,128]{3,2,1,0:T(8,128)(2,1)} %param.11), kind=kOutput, calls=%fused_computation.9 | convolution fusion | flops 8388608 | bytes 8585216 | tf_op jit(solution)/shard_map/mc,mcd->md/dot_general | solution.py:54
  386.0 5.7 %fusion.7 = f32[256,1,128]{2,1,0:T(1,128)S(1)} fusion(bf16[256,128,1]{1,2,0:T(2,128)(2,1)S(1)} %copy.11, bf16[256,2,128,128]{3,2,1,0:T(8,128)(2,1)} %param.11), kind=kOutput, calls=%fused_computation.11 | convolution fusion | flops 8388608 | bytes 8585216 | tf_op jit(solution)/shard_map/mc,mcd->md/dot_general | solution.py:57
  391.8 0.2 stack.2
  392.0 50.6 %all_to_all.5 = bf16[16,256,256]{2,1,0:T(8,128)(2,1)S(1)} all-to-all(bf16[16,256,256]{2,1,0:T(8,128)(2,1)S(1)} %stack.2), channel_id=1, replica_groups=mesh['pts'=16,'modes'=2] {'pts'}, dimensions={0} | all-to-all | bytes 4194304 | tf_op jit(solution)/shard_map/all_to_all | solution.py:62
  442.6 0.1 fusion.35
  442.8 26.5 %fusion.15 = bf16[4096,128]{1,0:T(8,128)(2,1)} fusion(bf16[4096,4096]{1,0:T(8,128)(2,1)} %get-tuple-element.10, bf16[4096,4096]{1,0:T(8,128)(2,1)} %get-tuple-element.9, bf16[4096,128]{1,0:T(8,128)(2,1)S(1)} %get-tuple-element.6, bf16[4096,128]{1,0:T(8,128)(2,1)S(1)} %get-tuple-element.5), kind=kOutput, calls=%fused_computation.19 | convolution fusion | flops 8728870912 | bytes 70254592 | tf_op jit(solution)/shard_map/dot_general | solution.py:66
  469.3 0.6 reduce_sum.9
  469.9 33.9 %psum.7 = f32[]{:T(128)} all-reduce(f32[]{:T(128)} %reduce_sum.9), channel_id=1, replica_groups=mesh['pts'=16,'modes'=2] {'pts'}, use_global_device_ids=true, to_apply=%region_3.0 | all-reduce | flops 1 | bytes 8 | tf_op jit(solution)/shard_map/psum | solution.py:24
  503.8 5.0 fusion.22
  (13 shorter events, 0.1 us)
Async XLA Ops:
  6.5 497.3 %copy-start = (bf16[128,128]{1,0:T(8,128)(2,1)S(1)}, bf16[128,128]{1,0:T(8,128)(2,1)}, u32[]{:S(2)}) copy-start(bf16[128,128]{1,0:T(8,128)(2,1)} %param.12) | copy-start | bytes 98308
  6.5 361.3 %reduce-scatter.3.cloned.1.call-start = ((), (), s32[]{:S(2)}) async-start(), calls=%async_computation.3 | async-start | bytes 2228224 | tf_op jit(solution)/shard_map/reduce_scatter | solution.py:39
  8.7 264.3 %copy-start.1 = (f32[4096]{0:T(1024)S(1)}, f32[4096]{0:T(1024)}, u32[]{:S(2)}) copy-start(f32[4096]{0:T(1024)} %param.9) | copy-start | bytes 49156
  8.7 264.3 %copy-start.2 = (bf16[4096,128]{1,0:T(8,128)(2,1)S(1)}, bf16[4096,128]{1,0:T(8,128)(2,1)}, u32[]{:S(2)}) copy-start(bf16[4096,128]{1,0:T(8,128)(2,1)} %param.7) | copy-start | bytes 3145732
  303.1 200.7 %reduce-scatter.5.cloned.1.call-start = ((), (), s32[]{:S(2)}) async-start(), calls=%async_computation.4 | async-start | bytes 1572864 | tf_op jit(solution)/shard_map/reduce_scatter | solution.py:67
  442.8 61.1 %copy-start.3 = (f32[128]{0:T(128)S(1)}, f32[128]{0:T(128)}, u32[]{:S(2)}) copy-start(f32[128]{0:T(128)} %param.13) | copy-start | bytes 1540
Sparse Core Ops, SparseCore 0:
  303.2 64.5 reduce-scatter.2
  469.4 20.8 reduce-scatter.4
